TPU v7x, 32 devices: a whole 2x2x4 slice. The times are simulated.
32 devices in a mesh: row: 8 (over z, x), col: 4 (over y, core).
Axes of the slice: x: 2, y: 2, z: 4, core: 2. Of those that a mesh axis runs over, the one named last changes fastest.
Arguments:
- matrix: float32 [32768, 2048], P('row', 'col'), may hold values from -6 to 6
- leaf_vectors: float32 [3, 32768, 128], P(None, ('row', 'col')), may hold values from -0.09375 to 0.09375
- leaf_factors: float32 [3, 1024, 128], P(None, ('row', 'col')), may hold values from -1.5 to 1.5
- tree_vectors: float32 [3, 1024, 128], P(None, ('row', 'col')), may hold values from -0.5 to 0.5
- tree_factors: float32 [3, 1024, 128], P(None, ('row', 'col')), may hold values from -0.875 to 0.875
Outputs:
- updated: float32 [32768, 2048], P('row', 'col')
All inputs are finite; a program needn't handle non-finite values.
Results may differ from a plain program's by a relative error of at most 0.0001.
Values sent between devices are 32-bit elements; how exact they have to be, the bound alone decides.
A program may use at most 128 MiB of HBM per device.

v0:
```python
import jax
import jax.numpy as jnp
from jax import lax
from jax.sharding import PartitionSpec as P


def swapped(block, axis, bit):
    count = lax.axis_size(axis)
    route = []
    for low in range(count):
        high = low | 1 << bit
        if high != low and high < count:
            route += [(low, high), (high, low)]
    return lax.ppermute(block, axis, route)


def transposed_dot(left, right):
    return lax.dot_general(left, right, (((0,), (0,)), ((), ())), precision=lax.Precision.HIGHEST)


def plain_dot(left, right):
    return jnp.dot(left, right, precision=lax.Precision.HIGHEST)


def local(matrix, leaf_vectors, leaf_factors, tree_vectors, tree_factors):
    block_width = leaf_vectors.shape[2]
    panel_count = leaf_vectors.shape[0]
    levels = lax.axis_size("row").bit_length() - 1
    row_index = lax.axis_index("row")
    node_vectors, node_factors = (
        lax.all_gather(tree_vectors, "col", axis=1, tiled=True),
        lax.all_gather(tree_factors, "col", axis=1, tiled=True),
    )
    node_factors = jnp.triu(node_factors)
    trailing = matrix
    for tick_index in range(panel_count):
        leaf_vec, leaf_fac = (
            lax.all_gather(leaf_vectors[tick_index], "col", axis=0, tiled=True),
            lax.all_gather(leaf_factors[tick_index], "col", axis=0, tiled=True),
        )
        leaf_fac = jnp.triu(leaf_fac)
        projected = transposed_dot(leaf_vec, trailing)
        scaled = transposed_dot(leaf_fac, projected)
        trailing = trailing - plain_dot(leaf_vec, scaled)
        top_rows = trailing[:block_width]
        own_vector = node_vectors[tick_index]
        own_factor = node_factors[tick_index]
        for tree_level in range(levels):
            stride = 1 << tree_level
            position = row_index % (2 * stride)
            is_upper = position == 0
            is_lower = position == stride
            partner, other_vector, other_factor = swapped(
                (top_rows, own_vector, own_factor), "row", tree_level
            )
            sel_vector = jnp.where(is_lower, own_vector, other_vector)
            sel_factor = jnp.where(is_lower, own_factor, other_factor)
            upper_rows = jnp.where(is_lower, partner, top_rows)
            lower_rows = jnp.where(is_lower, top_rows, partner)
            coupled = transposed_dot(
                sel_factor, upper_rows + transposed_dot(sel_vector, lower_rows)
            )
            change_rows = jnp.where(is_lower, plain_dot(sel_vector, coupled), coupled)
            top_rows = jnp.where(
                jnp.logical_or(is_upper, is_lower), top_rows - change_rows, top_rows
            )
        trailing = jnp.concatenate([top_rows, trailing[block_width:]], axis=0)
    return trailing


def solution(mesh):
    placed = (
        P("row", "col"),
        P(None, ("row", "col"), None),
        P(None, ("row", "col"), None),
        P(None, ("row", "col"), None),
        P(None, ("row", "col"), None),
    )
    return jax.shard_map(
        local, mesh=mesh, in_specs=placed, out_specs=P("row", "col"), check_vma=False
    )
```

profile of v0, /device:TPU:0, one launch (start us, length us, event | category | flops | bytes accessed | tf_op | source)
XLA Modules:
  0.0 254.3 jit_solution(7541880228211691032)
XLA Ops:
  6.5 2.6 %fusion.128 = (f32[1,1024,128]{2,1,0:T(8,128)}, f32[1,1024,128]{2,1,0:T(8,128)}, f32[1,1024,128]{2,1,0:T(8,128)}) fusion(f32[3,1024,128]{2,1,0:T(8,128)} %param.6), kind=kLoop, calls=%fused_computation.164 | loop fusion | bytes 3145728 | tf_op jit(solution)/shard_map/slice | solution.py:38
  9.2 7.1 %all_gather.26 = f32[3,128,128]{2,1,0:T(8,128)S(1)} all-gather(f32[3,32,128]{2,1,0:T(8,128)} %param.8), channel_id=1, replica_groups=mesh['row'=8,'col'=4] {'col'}, dimensions={1}, use_global_device_ids=true | all-gather | bytes 245760 | tf_op jit(solution)/shard_map/all_gather | solution.py:31
  16.3 1.7 collective-permute-start
  18.9 5.3 %all-gather = f32[1,128,128]{2,1,0:T(8,128)S(1)} all-gather(f32[1,32,128]{2,1,0:T(8,128)S(1)} %get-tuple-element.15), channel_id=2, replica_groups=mesh['row'=8,'col'=4] {'col'}, dimensions={1}, use_global_device_ids=true | all-gather | bytes 81920 | tf_op jit(solution)/shard_map/all_gather | solution.py:39
  24.2 8.9 %copy.6 = f32[4096,512]{0,1:T(8,128)} copy(f32[4096,512]{1,0:T(8,128)} %param.5) | data formatting | bytes 16777216 | tf_op args[0]
  33.3 5.6 %all_gather.27 = f32[3,128,128]{2,1,0:T(8,128)S(1)} all-gather(f32[3,32,128]{2,1,0:T(8,128)S(1)} %copy-done.9), channel_id=1, replica_groups=mesh['row'=8,'col'=4] {'col'}, dimensions={1}, use_global_device_ids=true | all-gather | bytes 245760 | tf_op jit(solution)/shard_map/all_gather | solution.py:32
  38.9 10.6 %fusion.7 = f32[128,512]{1,0:T(8,128)S(1)} fusion(f32[4096,512]{1,0:T(8,128)} %param.5, f32[1,4096,128]{2,1,0:T(8,128)} %all-gather.10.cloned.1.call-done), kind=kOutput, calls=%fused_computation.13 | convolution fusion | flops 3221225472 | bytes 10747904 | tf_op jit(solution)/shard_map/dot_general | solution.py:18
  50.0 7.5 %bitcast_subtract_fusion.2 = f32[4096,512]{0,1:T(8,128)S(1)} fusion(f32[4096,512]{0,1:T(8,128)S(1)} %copy-done.3, f32[128,512]{1,0:T(8,128)S(1)} %fusion.92, f32[1,4096,128]{2,1,0:T(8,128)S(1)} %copy-done.6), kind=kOutput, calls=%fused_computation.5 | convolution fusion | flops 3223322624 | bytes 19136512 | tf_op jit(solution)/shard_map/dot_general | solution.py:22
  57.5 3.4 %copy-done = f32[4096,512]{0,1:T(8,128)} copy-done((f32[4096,512]{0,1:T(8,128)}, f32[4096,512]{0,1:T(8,128)S(1)}, u32[]{:S(2)}) %copy-start) | copy-done | bytes 8388632
  61.4 1.7 collective-permute-start.1
  63.1 7.0 %collective-permute-done.2 = f32[128,512]{0,1:T(8,128)S(1)} collective-permute-done((f32[128,512]{0,1:T(8,128)S(1)}, f32[128,512]{0,1:T(8,128)S(1)}, u32[]{:S(2)}, u32[]{:S(2)}) %collective-permute-start.2) | collective-permute-done | bytes 262176 | tf_op jit(solution)/shard_map/ppermute | solution.py:14
  78.2 5.7 %collective-permute-done.3 = f32[128,128]{1,0:T(8,128)S(1)} collective-permute-done((f32[128,128]{1,0:T(8,128)S(1)}, f32[128,128]{1,0:T(8,128)S(1)}, u32[]{:S(2)}, u32[]{:S(2)}) %collective-permute-start.3) | collective-permute-done | bytes 65568 | tf_op jit(solution)/shard_map/ppermute | solution.py:14
  85.9 2.7 %collective-permute-start.8 = (f32[128,512]{0,1:T(8,128)S(1)}, f32[128,512]{0,1:T(8,128)S(1)}, u32[]{:S(2)}, u32[]{:S(2)}) collective-permute-start(f32[128,512]{0,1:T(8,128)S(1)} %fusion.24), channel_id=1, source_target_pairs={{0,16},{16,0},{4,20},{20,4},{8,24},{24,8},{12,28},{28,12},{1,17},{... | collective-permute-start | bytes 786440 | tf_op jit(solution)/shard_map/ppermute | solution.py:14
  88.9 2.7 %collective-permute-start.7 = (f32[128,128]{1,0:T(8,128)S(1)}, f32[128,128]{1,0:T(8,128)S(1)}, u32[]{:S(2)}, u32[]{:S(2)}) collective-permute-start(f32[128,128]{1,0:T(8,128)S(1)} %get-tuple-element.10), channel_id=1, source_target_pairs={{0,16},{16,0},{4,20},{20,4},{8,24},{24,8},{12,28},{28,12},{1,17},{... | collective-permute-start | bytes 196616 | tf_op jit(solution)/shard_map/ppermute | solution.py:14
  91.6 5.4 %all-gather.2 = f32[1,128,128]{2,1,0:T(8,128)S(1)} all-gather(f32[1,32,128]{2,1,0:T(8,128)S(1)} %get-tuple-element.16), channel_id=4, replica_groups=mesh['row'=8,'col'=4] {'col'}, dimensions={1}, use_global_device_ids=true | all-gather | bytes 81920 | tf_op jit(solution)/shard_map/all_gather | solution.py:39
  97.0 7.4 %slice.75 = f32[3968,512]{0,1:T(8,128)} slice(f32[4096,512]{0,1:T(8,128)} %copy-done), slice={[128:4096], [0:512]} | slice | bytes 16252928 | tf_op jit(solution)/shard_map/slice | solution.py:67
  106.0 9.5 %fusion.1 = f32[512,128]{1,0:T(8,128)S(1)} fusion(f32[3968,512]{0,1:T(8,128)} %slice.75, f32[128,512]{0,1:T(8,128)S(1)} %fusion.22, f32[1,4096,128]{2,1,0:T(8,128)} %all-gather.12.cloned.1.call-done), kind=kOutput, calls=%fused_computation.7 | convolution fusion | flops 3223322624 | bytes 10747904 | tf_op jit(solution)/shard_map/dot_general | solution.py:18
  116.0 7.7 %bitcast_subtract_fusion.1 = f32[4096,512]{0,1:T(8,128)S(1)} fusion(f32[3968,512]{0,1:T(8,128)S(1)} %copy-done.5, f32[128,512]{0,1:T(8,128)S(1)} %fusion.22, f32[128,512]{1,0:T(8,128)S(1)} %fusion.91, f32[1,4096,128]{2,1,0:T(8,128)S(1)} %copy-done.7), kind=kOutput, calls=%fused_computation.4 | convolution fusion | flops 3225419776 | bytes 19136512 | tf_op jit(solution)/shard_map/dot_general | solution.py:22
  126.5 7.9 %collective-permute-done.9 = f32[128,128]{1,0:T(8,128)S(1)} collective-permute-done((f32[128,128]{1,0:T(8,128)S(1)}, f32[128,128]{1,0:T(8,128)S(1)}, u32[]{:S(2)}, u32[]{:S(2)}) %collective-permute-start.9) | collective-permute-done | bytes 65568 | tf_op jit(solution)/shard_map/ppermute | solution.py:14
  141.0 6.2 %collective-permute-done.12 = f32[128,128]{1,0:T(8,128)S(1)} collective-permute-done((f32[128,128]{1,0:T(8,128)S(1)}, f32[128,128]{1,0:T(8,128)S(1)}, u32[]{:S(2)}, u32[]{:S(2)}) %collective-permute-start.12) | collective-permute-done | bytes 65568 | tf_op jit(solution)/shard_map/ppermute | solution.py:14
  153.5 5.6 %all-gather.4 = f32[1,128,128]{2,1,0:T(8,128)S(1)} all-gather(f32[1,32,128]{2,1,0:T(8,128)S(1)} %get-tuple-element.14), channel_id=6, replica_groups=mesh['row'=8,'col'=4] {'col'}, dimensions={1}, use_global_device_ids=true | all-gather | bytes 81920 | tf_op jit(solution)/shard_map/all_gather | solution.py:39
  159.1 7.0 %slice.79 = f32[3968,512]{0,1:T(8,128)} slice(f32[4096,512]{0,1:T(8,128)} %copy-done.2), slice={[128:4096], [0:512]} | slice | bytes 16252928 | tf_op jit(solution)/shard_map/slice | solution.py:67
  169.3 9.6 %fusion = f32[512,128]{1,0:T(8,128)S(1)} fusion(f32[3968,512]{0,1:T(8,128)} %slice.79, f32[128,512]{0,1:T(8,128)S(1)} %fusion.16, f32[1,4096,128]{2,1,0:T(8,128)} %all-gather.14.cloned.1.call-done), kind=kOutput, calls=%fused_computation.6 | convolution fusion | flops 3223322624 | bytes 10747904 | tf_op jit(solution)/shard_map/dot_general | solution.py:18
  179.5 7.7 %bitcast_subtract_fusion = f32[4096,512]{0,1:T(8,128)S(1)} fusion(f32[3968,512]{0,1:T(8,128)S(1)} %copy-done.4, f32[128,512]{0,1:T(8,128)S(1)} %fusion.16, f32[128,512]{1,0:T(8,128)S(1)} %fusion.90, f32[1,4096,128]{2,1,0:T(8,128)S(1)} %copy-done.8), kind=kOutput, calls=%fused_computation.3 | convolution fusion | flops 3225419776 | bytes 19136512 | tf_op jit(solution)/shard_map/dot_general | solution.py:22
  190.0 6.6 %collective-permute-done.18 = f32[128,128]{1,0:T(8,128)S(1)} collective-permute-done((f32[128,128]{1,0:T(8,128)S(1)}, f32[128,128]{1,0:T(8,128)S(1)}, u32[]{:S(2)}, u32[]{:S(2)}) %collective-permute-start.18) | collective-permute-done | bytes 65568 | tf_op jit(solution)/shard_map/ppermute | solution.py:14
  203.1 6.1 %collective-permute-done.21 = f32[128,128]{1,0:T(8,128)S(1)} collective-permute-done((f32[128,128]{1,0:T(8,128)S(1)}, f32[128,128]{1,0:T(8,128)S(1)}, u32[]{:S(2)}, u32[]{:S(2)}) %collective-permute-start.21) | collective-permute-done | bytes 65568 | tf_op jit(solution)/shard_map/ppermute | solution.py:14
  211.0 2.0 collective-permute-start.26
  214.0 1.9 collective-permute-start.25
  215.9 7.0 %slice.83 = f32[3968,512]{0,1:T(8,128)} slice(f32[4096,512]{0,1:T(8,128)} %copy-done.1), slice={[128:4096], [0:512]} | slice | bytes 16252928 | tf_op jit(solution)/shard_map/slice | solution.py:67
  222.9 6.2 %collective-permute-done.24 = f32[128,128]{1,0:T(8,128)S(1)} collective-permute-done((f32[128,128]{1,0:T(8,128)S(1)}, f32[128,128]{1,0:T(8,128)S(1)}, u32[]{:S(2)}, u32[]{:S(2)}) %collective-permute-start.24) | collective-permute-done | bytes 65568 | tf_op jit(solution)/shard_map/ppermute | solution.py:14
  231.0 7.6 %pad_maximum_fusion.2 = f32[4096,512]{0,1:T(8,128)} fusion(f32[3968,512]{0,1:T(8,128)} %slice.83, f32[128,512]{0,1:T(8,128)S(1)} %fusion.10), kind=kLoop, calls=%fused_computation.2 | loop fusion | flops 2097152 | bytes 16777216 | tf_op jit(solution)/shard_map/concatenate | solution.py:67
  238.7 8.9 %copy.25 = f32[4096,512]{1,0:T(8,128)} copy(f32[4096,512]{0,1:T(8,128)} %pad_maximum_fusion.2) | data formatting | bytes 16777216 | tf_op jit(solution)/shard_map/concatenate | solution.py:67
  (117 shorter events, 47.4 us)
Async XLA Ops:
  6.5 32.3 %all-gather.10.cloned.1.call-start = ((), (), s32[]{:S(2)}) async-start(), calls=%async_computation | async-start | bytes 2621440 | tf_op jit(solution)/shard_map/all_gather | solution.py:38
  9.1 96.8 %all-gather.12.cloned.1.call-start = ((), (), s32[]{:S(2)}) async-start(), calls=%async_computation.1 | async-start | bytes 2621440 | tf_op jit(solution)/shard_map/all_gather | solution.py:38
  16.3 46.8 %collective-permute-start = (f32[128,128]{1,0:T(8,128)S(1)}, f32[128,128]{1,0:T(8,128)S(1)}, u32[]{:S(2)}, u32[]{:S(2)}) collective-permute-start(f32[128,128]{1,0:T(8,128)S(1)} %get-tuple-element.13), channel_id=1, source_target_pairs={{0,4},{4,0},{8,12},{12,8},{16,20},{20,16},{24,28},{28,24},{1,5},{5... | collective-permute-start | bytes 196616 | tf_op jit(solution)/shard_map/ppermute | solution.py:14
  18.1 151.3 %all-gather.14.cloned.1.call-start = ((), (), s32[]{:S(2)}) async-start(), calls=%async_computation.2 | async-start | bytes 2621440 | tf_op jit(solution)/shard_map/all_gather | solution.py:38
  38.9 11.1 %copy-start.6 = (f32[1,4096,128]{2,1,0:T(8,128)S(1)}, f32[1,4096,128]{2,1,0:T(8,128)}, u32[]{:S(2)}) copy-start(f32[1,4096,128]{2,1,0:T(8,128)} %all-gather.10.cloned.1.call-done) | copy-start | bytes 6291460
  60.9 9.2 %collective-permute-start.2 = (f32[128,512]{0,1:T(8,128)S(1)}, f32[128,512]{0,1:T(8,128)S(1)}, u32[]{:S(2)}, u32[]{:S(2)}) collective-permute-start(f32[128,512]{0,1:T(8,128)S(1)} %slice.72), channel_id=1, source_target_pairs={{0,4},{4,0},{8,12},{12,8},{16,20},{20,16},{24,28},{28,24},{1,5},{5... | collective-permute-start | bytes 786440 | tf_op jit(solution)/shard_map/ppermute | solution.py:14
  61.4 10.1 %collective-permute-start.1 = (f32[128,128]{1,0:T(8,128)S(1)}, f32[128,128]{1,0:T(8,128)S(1)}, u32[]{:S(2)}, u32[]{:S(2)}) collective-permute-start(f32[128,128]{1,0:T(8,128)S(1)} %get-tuple-element.10), channel_id=1, source_target_pairs={{0,4},{4,0},{8,12},{12,8},{16,20},{20,16},{24,28},{28,24},{1,5},{5... | collective-permute-start | bytes 196616 | tf_op jit(solution)/shard_map/ppermute | solution.py:14
  74.5 9.4 %collective-permute-start.5 = (f32[128,512]{0,1:T(8,128)S(1)}, f32[128,512]{0,1:T(8,128)S(1)}, u32[]{:S(2)}, u32[]{:S(2)}) collective-permute-start(f32[128,512]{0,1:T(8,128)S(1)} %fusion.26), channel_id=1, source_target_pairs={{0,8},{8,0},{4,12},{12,4},{16,24},{24,16},{20,28},{28,20},{1,9},{9... | collective-permute-start | bytes 786440 | tf_op jit(solution)/shard_map/ppermute | solution.py:14
  76.2 7.8 %collective-permute-start.3 = (f32[128,128]{1,0:T(8,128)S(1)}, f32[128,128]{1,0:T(8,128)S(1)}, u32[]{:S(2)}, u32[]{:S(2)}) collective-permute-start(f32[128,128]{1,0:T(8,128)S(1)} %get-tuple-element.13), channel_id=1, source_target_pairs={{0,8},{8,0},{4,12},{12,4},{16,24},{24,16},{20,28},{28,20},{1,9},{9... | collective-permute-start | bytes 196616 | tf_op jit(solution)/shard_map/ppermute | solution.py:14
  76.6 8.0 %collective-permute-start.4 = (f32[128,128]{1,0:T(8,128)S(1)}, f32[128,128]{1,0:T(8,128)S(1)}, u32[]{:S(2)}, u32[]{:S(2)}) collective-permute-start(f32[128,128]{1,0:T(8,128)S(1)} %get-tuple-element.10), channel_id=1, source_target_pairs={{0,8},{8,0},{4,12},{12,4},{16,24},{24,16},{20,28},{28,20},{1,9},{9... | collective-permute-start | bytes 196616 | tf_op jit(solution)/shard_map/ppermute | solution.py:14
  85.9 18.5 %collective-permute-start.8 = (f32[128,512]{0,1:T(8,128)S(1)}, f32[128,512]{0,1:T(8,128)S(1)}, u32[]{:S(2)}, u32[]{:S(2)}) collective-permute-start(f32[128,512]{0,1:T(8,128)S(1)} %fusion.24), channel_id=1, source_target_pairs={{0,16},{16,0},{4,20},{20,4},{8,24},{24,8},{12,28},{28,12},{1,17},{... | collective-permute-start | bytes 786440 | tf_op jit(solution)/shard_map/ppermute | solution.py:14
  88.6 15.8 %collective-permute-start.6 = (f32[128,128]{1,0:T(8,128)S(1)}, f32[128,128]{1,0:T(8,128)S(1)}, u32[]{:S(2)}, u32[]{:S(2)}) collective-permute-start(f32[128,128]{1,0:T(8,128)S(1)} %get-tuple-element.13), channel_id=1, source_target_pairs={{0,16},{16,0},{4,20},{20,4},{8,24},{24,8},{12,28},{28,12},{1,17},{... | collective-permute-start | bytes 196616 | tf_op jit(solution)/shard_map/ppermute | solution.py:14
  88.9 15.9 %collective-permute-start.7 = (f32[128,128]{1,0:T(8,128)S(1)}, f32[128,128]{1,0:T(8,128)S(1)}, u32[]{:S(2)}, u32[]{:S(2)}) collective-permute-start(f32[128,128]{1,0:T(8,128)S(1)} %get-tuple-element.10), channel_id=1, source_target_pairs={{0,16},{16,0},{4,20},{20,4},{8,24},{24,8},{12,28},{28,12},{1,17},{... | collective-permute-start | bytes 196616 | tf_op jit(solution)/shard_map/ppermute | solution.py:14
  123.7 11.5 %copy-start.2 = (f32[4096,512]{0,1:T(8,128)}, f32[4096,512]{0,1:T(8,128)S(1)}, u32[]{:S(2)}) copy-start(f32[4096,512]{0,1:T(8,128)S(1)} %bitcast_subtract_fusion.1) | copy-start | bytes 25165828
  123.8 10.6 %collective-permute-start.11 = (f32[128,512]{0,1:T(8,128)S(1)}, f32[128,512]{0,1:T(8,128)S(1)}, u32[]{:S(2)}, u32[]{:S(2)}) collective-permute-start(f32[128,512]{0,1:T(8,128)S(1)} %slice.76), channel_id=1, source_target_pairs={{0,4},{4,0},{8,12},{12,8},{16,20},{20,16},{24,28},{28,24},{1,5},{5... | collective-permute-start | bytes 786440 | tf_op jit(solution)/shard_map/ppermute | solution.py:14
  124.4 9.9 %collective-permute-start.9 = (f32[128,128]{1,0:T(8,128)S(1)}, f32[128,128]{1,0:T(8,128)S(1)}, u32[]{:S(2)}, u32[]{:S(2)}) collective-permute-start(f32[128,128]{1,0:T(8,128)S(1)} %get-tuple-element.12), channel_id=1, source_target_pairs={{0,4},{4,0},{8,12},{12,8},{16,20},{20,16},{24,28},{28,24},{1,5},{5... | collective-permute-start | bytes 196616 | tf_op jit(solution)/shard_map/ppermute | solution.py:14
  125.9 9.3 %collective-permute-start.10 = (f32[128,128]{1,0:T(8,128)S(1)}, f32[128,128]{1,0:T(8,128)S(1)}, u32[]{:S(2)}, u32[]{:S(2)}) collective-permute-start(f32[128,128]{1,0:T(8,128)S(1)} %get-tuple-element.9), channel_id=1, source_target_pairs={{0,4},{4,0},{8,12},{12,8},{16,20},{20,16},{24,28},{28,24},{1,5},{5... | collective-permute-start | bytes 196616 | tf_op jit(solution)/shard_map/ppermute | solution.py:14
  137.3 9.9 %collective-permute-start.14 = (f32[128,512]{0,1:T(8,128)S(1)}, f32[128,512]{0,1:T(8,128)S(1)}, u32[]{:S(2)}, u32[]{:S(2)}) collective-permute-start(f32[128,512]{0,1:T(8,128)S(1)} %fusion.20), channel_id=1, source_target_pairs={{0,8},{8,0},{4,12},{12,4},{16,24},{24,16},{20,28},{28,20},{1,9},{9... | collective-permute-start | bytes 786440 | tf_op jit(solution)/shard_map/ppermute | solution.py:14
  139.0 8.2 %collective-permute-start.12 = (f32[128,128]{1,0:T(8,128)S(1)}, f32[128,128]{1,0:T(8,128)S(1)}, u32[]{:S(2)}, u32[]{:S(2)}) collective-permute-start(f32[128,128]{1,0:T(8,128)S(1)} %get-tuple-element.12), channel_id=1, source_target_pairs={{0,8},{8,0},{4,12},{12,4},{16,24},{24,16},{20,28},{28,20},{1,9},{9... | collective-permute-start | bytes 196616 | tf_op jit(solution)/shard_map/ppermute | solution.py:14
  139.4 8.5 %collective-permute-start.13 = (f32[128,128]{1,0:T(8,128)S(1)}, f32[128,128]{1,0:T(8,128)S(1)}, u32[]{:S(2)}, u32[]{:S(2)}) collective-permute-start(f32[128,128]{1,0:T(8,128)S(1)} %get-tuple-element.9), channel_id=1, source_target_pairs={{0,8},{8,0},{4,12},{12,4},{16,24},{24,16},{20,28},{28,20},{1,9},{9... | collective-permute-start | bytes 196616 | tf_op jit(solution)/shard_map/ppermute | solution.py:14
  149.1 18.3 %collective-permute-start.17 = (f32[128,512]{0,1:T(8,128)S(1)}, f32[128,512]{0,1:T(8,128)S(1)}, u32[]{:S(2)}, u32[]{:S(2)}) collective-permute-start(f32[128,512]{0,1:T(8,128)S(1)} %fusion.18), channel_id=1, source_target_pairs={{0,16},{16,0},{4,20},{20,4},{8,24},{24,8},{12,28},{28,12},{1,17},{... | collective-permute-start | bytes 786440 | tf_op jit(solution)/shard_map/ppermute | solution.py:14
  150.5 16.9 %collective-permute-start.15 = (f32[128,128]{1,0:T(8,128)S(1)}, f32[128,128]{1,0:T(8,128)S(1)}, u32[]{:S(2)}, u32[]{:S(2)}) collective-permute-start(f32[128,128]{1,0:T(8,128)S(1)} %get-tuple-element.12), channel_id=1, source_target_pairs={{0,16},{16,0},{4,20},{20,4},{8,24},{24,8},{12,28},{28,12},{1,17},{... | collective-permute-start | bytes 196616 | tf_op jit(solution)/shard_map/ppermute | solution.py:14
  152.1 16.0 %collective-permute-start.16 = (f32[128,128]{1,0:T(8,128)S(1)}, f32[128,128]{1,0:T(8,128)S(1)}, u32[]{:S(2)}, u32[]{:S(2)}) collective-permute-start(f32[128,128]{1,0:T(8,128)S(1)} %get-tuple-element.9), channel_id=1, source_target_pairs={{0,16},{16,0},{4,20},{20,4},{8,24},{24,8},{12,28},{28,12},{1,17},{... | collective-permute-start | bytes 196616 | tf_op jit(solution)/shard_map/ppermute | solution.py:14
  187.2 9.4 %collective-permute-start.20 = (f32[128,512]{0,1:T(8,128)S(1)}, f32[128,512]{0,1:T(8,128)S(1)}, u32[]{:S(2)}, u32[]{:S(2)}) collective-permute-start(f32[128,512]{0,1:T(8,128)S(1)} %slice.80), channel_id=1, source_target_pairs={{0,4},{4,0},{8,12},{12,8},{16,20},{20,16},{24,28},{28,24},{1,5},{5... | collective-permute-start | bytes 786440 | tf_op jit(solution)/shard_map/ppermute | solution.py:14
  187.9 8.7 %collective-permute-start.18 = (f32[128,128]{1,0:T(8,128)S(1)}, f32[128,128]{1,0:T(8,128)S(1)}, u32[]{:S(2)}, u32[]{:S(2)}) collective-permute-start(f32[128,128]{1,0:T(8,128)S(1)} %get-tuple-element.11), channel_id=1, source_target_pairs={{0,4},{4,0},{8,12},{12,8},{16,20},{20,16},{24,28},{28,24},{1,5},{5... | collective-permute-start | bytes 196616 | tf_op jit(solution)/shard_map/ppermute | solution.py:14
  189.3 8.0 %collective-permute-start.19 = (f32[128,128]{1,0:T(8,128)S(1)}, f32[128,128]{1,0:T(8,128)S(1)}, u32[]{:S(2)}, u32[]{:S(2)}) collective-permute-start(f32[128,128]{1,0:T(8,128)S(1)} %get-tuple-element.8), channel_id=1, source_target_pairs={{0,4},{4,0},{8,12},{12,8},{16,20},{20,16},{24,28},{28,24},{1,5},{5... | collective-permute-start | bytes 196616 | tf_op jit(solution)/shard_map/ppermute | solution.py:14
  199.4 9.7 %collective-permute-start.23 = (f32[128,512]{0,1:T(8,128)S(1)}, f32[128,512]{0,1:T(8,128)S(1)}, u32[]{:S(2)}, u32[]{:S(2)}) collective-permute-start(f32[128,512]{0,1:T(8,128)S(1)} %fusion.14), channel_id=1, source_target_pairs={{0,8},{8,0},{4,12},{12,4},{16,24},{24,16},{20,28},{28,20},{1,9},{9... | collective-permute-start | bytes 786440 | tf_op jit(solution)/shard_map/ppermute | solution.py:14
  201.0 8.1 %collective-permute-start.21 = (f32[128,128]{1,0:T(8,128)S(1)}, f32[128,128]{1,0:T(8,128)S(1)}, u32[]{:S(2)}, u32[]{:S(2)}) collective-permute-start(f32[128,128]{1,0:T(8,128)S(1)} %get-tuple-element.11), channel_id=1, source_target_pairs={{0,8},{8,0},{4,12},{12,4},{16,24},{24,16},{20,28},{28,20},{1,9},{9... | collective-permute-start | bytes 196616 | tf_op jit(solution)/shard_map/ppermute | solution.py:14
  201.5 8.3 %collective-permute-start.22 = (f32[128,128]{1,0:T(8,128)S(1)}, f32[128,128]{1,0:T(8,128)S(1)}, u32[]{:S(2)}, u32[]{:S(2)}) collective-permute-start(f32[128,128]{1,0:T(8,128)S(1)} %get-tuple-element.8), channel_id=1, source_target_pairs={{0,8},{8,0},{4,12},{12,4},{16,24},{24,16},{20,28},{28,20},{1,9},{9... | collective-permute-start | bytes 196616 | tf_op jit(solution)/shard_map/ppermute | solution.py:14
  211.0 18.1 %collective-permute-start.26 = (f32[128,512]{0,1:T(8,128)S(1)}, f32[128,512]{0,1:T(8,128)S(1)}, u32[]{:S(2)}, u32[]{:S(2)}) collective-permute-start(f32[128,512]{0,1:T(8,128)S(1)} %fusion.12), channel_id=1, source_target_pairs={{0,16},{16,0},{4,20},{20,4},{8,24},{24,8},{12,28},{28,12},{1,17},{... | collective-permute-start | bytes 786440 | tf_op jit(solution)/shard_map/ppermute | solution.py:14
  213.0 16.1 %collective-permute-start.24 = (f32[128,128]{1,0:T(8,128)S(1)}, f32[128,128]{1,0:T(8,128)S(1)}, u32[]{:S(2)}, u32[]{:S(2)}) collective-permute-start(f32[128,128]{1,0:T(8,128)S(1)} %get-tuple-element.11), channel_id=1, source_target_pairs={{0,16},{16,0},{4,20},{20,4},{8,24},{24,8},{12,28},{28,12},{1,17},{... | collective-permute-start | bytes 196616 | tf_op jit(solution)/shard_map/ppermute | solution.py:14
  214.0 15.8 %collective-permute-start.25 = (f32[128,128]{1,0:T(8,128)S(1)}, f32[128,128]{1,0:T(8,128)S(1)}, u32[]{:S(2)}, u32[]{:S(2)}) collective-permute-start(f32[128,128]{1,0:T(8,128)S(1)} %get-tuple-element.8), channel_id=1, source_target_pairs={{0,16},{16,0},{4,20},{20,4},{8,24},{24,8},{12,28},{28,12},{1,17},{... | collective-permute-start | bytes 196616 | tf_op jit(solution)/shard_map/ppermute | solution.py:14
  (8 other events, 73.9 us)
Sparse Core Ops, SparseCore 0:
  9.3 25.6 all-gather.9
  36.5 22.5 all-gather.11
  91.7 21.0 all-gather.13
where the time goes:
time: 259 us; the launch traced here: 254 us
  matrix products  71.5 us (28%)
  waiting for transfers between devices  49.6 us (19%)
  local copies, waits for them, and re-layouts  47.3 us (18%)
  starting transfers between devices  35.3 us (14%)
  blocking collectives  29.1 us (11%)
  between operations  13.9 us (5%)
  other arithmetic  7.73 us (3%)
    ppermute x27, waiting for transfers between devices, swapped(): return lax.ppermute(block, axis, route)  49.5 us
    dot_general x24, matrix products, transposed_dot(): lax.dot_general(left, right, (((0,), (0,)), ((), ())), precision=lax.Prec...  40.3 us
    ppermute x27, starting transfers between devices, swapped(): return lax.ppermute(block, axis, route)  35.2 us
    dot_general x12, matrix products, plain_dot(): return jnp.dot(left, right, precision=lax.Precision.HIGHEST)  31.1 us
    slice x3, local copies, waits for them, and re-layouts, local(): trailing = jnp.concatenate([top_rows, trailing[block_width:]], axis=0)  21.4 us
    all_gather x3, blocking collectives, local(): lax.all_gather(leaf_factors[tick_index], 'col', axis=0, tiled=True)  16.4 us
    unnamed x21, local copies, waits for them, and re-layouts  12.4 us
    concatenate x1, local copies, waits for them, and re-layouts, local(): trailing = jnp.concatenate([top_rows, trailing[block_width:]], axis=0)  8.94 us
  transfers between devices with their start and end apart: 30, of which 15 were waited for; matrix products, arithmetic and copies ran while one was open for 32% of the time, Pallas kernels for 0%

commit v1 on v0

v1 whole, which is shorter than its diff:
```python
import functools

import jax
import jax.numpy as jnp
from jax import lax
from jax.experimental import pallas as pl
from jax.experimental.pallas import tpu as pltpu
from jax.sharding import PartitionSpec as P

MESH = pl.DeviceIdType.MESH
F32 = jnp.float32
BF16 = jnp.bfloat16
TILE = 512
CHUNKS = 2


def split(x):
    high = x.astype(BF16)
    return high, (x - high.astype(F32)).astype(BF16)


def mm(x, y, contract_x):
    return lax.dot_general(
        x, y, (((contract_x,), (0,)), ((), ())), preferred_element_type=F32
    )


def dot3(x, y, contract_x):
    x_high, x_low = split(x)
    y_high, y_low = split(y)
    return (
        mm(x_high, y_high, contract_x)
        + mm(x_low, y_high, contract_x)
        + mm(x_high, y_low, contract_x)
    )


def upper_triangle(x):
    row = lax.broadcasted_iota(jnp.int32, x.shape, 0)
    col = lax.broadcasted_iota(jnp.int32, x.shape, 1)
    return jnp.where(row <= col, x, 0.0)


def low_bit(mask):
    return mask & -mask


def kernel(
    n_row, n_col,
    a_in, v_in, l_in, y_in, s_in, o_ref,
    a, v, vc, small, lower_s, top, proj, w_cat, w_low, sent, got,
    a_sem, v_own_sem, v_send, v_recv, small_own, small_send, small_recv,
    s_send, s_recv, x_send, x_recv, o_sem, o_top_sem,
):
    panels, shard, width = v_in.shape
    rows, cols = a_in.shape
    part = l_in.shape[1]
    levels = n_row.bit_length() - 1
    tiles = rows // TILE
    chunk = cols // CHUNKS
    r = lax.axis_index("row")
    c = lax.axis_index("col")

    def partner(mask):
        bits = c
        for bit in range(n_col.bit_length() - 1):
            if mask >> bit & 1:
                bits = bits + (1 << bit) - 2 * (1 << bit) * ((bits // (1 << bit)) % 2)
        return bits

    def row_partner(level):
        step = 1 << level
        return r + step - 2 * step * ((r // step) % 2)

    def block_rows(mask):
        return pl.ds(pl.multiple_of(partner(mask) * shard, shard), shard)

    def part_rows(mask):
        return pl.ds(pl.multiple_of(partner(mask) * part, part), part)

    def a_copy(mask):
        return pltpu.make_async_copy(
            a_in.at[block_rows(mask)], a.at[block_rows(mask)], a_sem.at[mask]
        )

    def v_own(k):
        return pltpu.make_async_copy(v_in.at[k], v.at[k, block_rows(0)], v_own_sem.at[k])

    def v_copy(k, mask):
        bit = low_bit(mask)
        held = mask ^ bit
        source = v_in.at[k] if held == 0 else v.at[k, block_rows(held)]
        return pltpu.make_async_remote_copy(
            src_ref=source,
            dst_ref=v.at[k, block_rows(held)],
            send_sem=v_send.at[k, mask],
            recv_sem=v_recv.at[k, mask],
            device_id={"row": r, "col": partner(bit)},
            device_id_type=MESH,
        )

    def small_local(which, source):
        return pltpu.make_async_copy(
            source, small.at[which, :, part_rows(0)], small_own.at[which]
        )

    def small_copy(which, source, mask):
        return pltpu.make_async_remote_copy(
            src_ref=source,
            dst_ref=small.at[which, :, part_rows(0)],
            send_sem=small_send.at[which, mask],
            recv_sem=small_recv.at[which, mask],
            device_id={"row": r, "col": partner(mask)},
            device_id_type=MESH,
        )

    def s_copy(level):
        return pltpu.make_async_remote_copy(
            src_ref=small.at[2],
            dst_ref=lower_s.at[level],
            send_sem=s_send.at[level],
            recv_sem=s_recv.at[level],
            device_id={"row": row_partner(level), "col": c},
            device_id_type=MESH,
        )

    def x_copy(k, level, piece):
        return pltpu.make_async_remote_copy(
            src_ref=sent.at[k, level, piece],
            dst_ref=got.at[k, level, piece],
            send_sem=x_send.at[k, level, piece],
            recv_sem=x_recv.at[k, level, piece],
            device_id={"row": row_partner(level), "col": c},
            device_id_type=MESH,
        )

    def is_lower(level):
        return r % (2 << level) == 1 << level

    def is_upper(level):
        return r % (2 << level) == 0

    def takes_part(level):
        return r % (1 << level) == 0

    masks = range(1, n_col)
    small_in = (l_in, y_in, s_in)

    for mask in range(n_col):
        a_copy(mask).start()
    for k in range(panels):
        v_own(k).start()
    for which in range(3):
        small_local(which, small_in[which]).start()

    barrier = pltpu.get_barrier_semaphore()
    for mask in masks:
        pl.semaphore_signal(
            barrier, inc=1, device_id={"row": r, "col": partner(mask)}, device_id_type=MESH
        )
    for level in range(levels):
        pl.semaphore_signal(
            barrier, inc=1, device_id={"row": row_partner(level), "col": c}, device_id_type=MESH
        )
    pl.semaphore_wait(barrier, n_col - 1 + levels)

    def start_far(k):
        for mask in masks:
            if mask == low_bit(mask) and mask > 1:
                v_copy(k, mask).start()

    def start_near(k):
        if n_col > 1:
            v_copy(k, 1).start()

    start_near(0)
    start_far(0)
    for which in range(3):
        for mask in masks:
            small_copy(which, small_in[which], mask).start()
    for k in range(1, panels):
        start_near(k)

    def project(k, mask):
        base = partner(mask) * shard

        def step(t, carry):
            at = pl.ds(pl.multiple_of(base + t * TILE, TILE), TILE)
            v_high, v_low = split(v[k, at])
            both = jnp.concatenate([v_high, v_low], axis=1)
            vc[at, :] = both
            a_high, a_low = split(a[at, :])
            out = mm(both, a_high, 0)
            proj[...] += out[:width] + out[width:] + mm(v_high, a_low, 0)
            return carry

        lax.fori_loop(0, shard // TILE, step, 0)

    def update(first, last, final):
        def step(t, carry):
            at = pl.ds(pl.multiple_of(t * TILE, TILE), TILE)
            both = vc[at, :]
            a[at, :] = a[at, :] - (
                mm(both, w_cat[...], 1) + mm(both[:, :width], w_low[...], 1)
            )
            if final:
                @pl.when(t > 0)
                def _():
                    pltpu.make_async_copy(a.at[at], o_ref.at[at], o_sem.at[t]).start()
            return carry

        lax.fori_loop(first, last, step, 0)

    def columns(piece):
        return pl.ds(piece * chunk, chunk)

    def send_level(k, level, piece):
        @pl.when(is_lower(level))
        def _():
            sent[k, level, piece] = dot3(small[1, k], top[:, columns(piece)], 0)

        @pl.when(is_upper(level))
        def _():
            sent[k, level, piece] = top[:, columns(piece)]

        @pl.when(takes_part(level))
        def _():
            x_copy(k, level, piece).start()

    def take_level(k, level, piece):
        @pl.when(takes_part(level))
        def _():
            x_copy(k, level, piece).wait_recv()

        @pl.when(is_lower(level))
        def _():
            total = sent[k, level, piece] + got[k, level, piece]
            coupled = dot3(upper_triangle(small[2, k]), total, 0)
            top[:, columns(piece)] -= dot3(small[1, k], coupled, 1)

        @pl.when(is_upper(level))
        def _():
            total = sent[k, level, piece] + got[k, level, piece]
            top[:, columns(piece)] -= dot3(upper_triangle(lower_s[level, k]), total, 0)

    def receive(k, mask):
        v_copy(k, mask).wait_recv()
        bit = 1
        while bit < low_bit(mask):
            v_copy(k, mask | bit).start()
            bit *= 2

    last_direct = n_col // 2
    order = [mask for mask in masks if mask == low_bit(mask)]
    order += [mask for mask in masks if mask != low_bit(mask)]

    proj[...] = jnp.zeros_like(proj)
    a_copy(0).wait()
    v_own(0).wait()
    project(0, 0)

    for k in range(panels):
        for mask in order:
            receive(k, mask)
            if mask == last_direct and k + 1 < panels:
                start_far(k + 1)
            if k == 0:
                a_copy(mask).wait()
            project(k, mask)
        if k == 0:
            top[...] = a[:width, :]
            for which in range(3):
                small_local(which, small_in[which]).wait()
                for mask in masks:
                    small_copy(which, small_in[which], mask).wait_recv()
            for level in range(levels):
                @pl.when(is_lower(level))
                def _():
                    s_copy(level).start()
        else:
            v_high, v_low = split(v[k, pl.ds(0, width)])
            t_high, t_low = split(top[...])
            proj[...] += mm(v_high, t_high, 0) + mm(v_low, t_high, 0) + mm(v_high, t_low, 0)

        w = dot3(upper_triangle(small[0, k]), proj[...], 0)
        w_high, w_small = split(w)
        w_cat[...] = jnp.concatenate([w_high, w_high], axis=0)
        w_low[...] = w_small
        head = vc[pl.ds(0, width), :]
        top[...] -= mm(head, w_cat[...], 1) + mm(head[:, :width], w_low[...], 1)

        for piece in range(CHUNKS):
            send_level(k, 0, piece)
        if k == 0:
            for level in range(levels):
                @pl.when(is_upper(level))
                def _():
                    s_copy(level).wait_recv()
        final = k == panels - 1
        for level in range(levels):
            update(tiles * level // levels, tiles * (level + 1) // levels, final)
            if level == levels - 1:
                if final:
                    rest = pl.ds(width, TILE - width)
                    pltpu.make_async_copy(a.at[rest], o_ref.at[rest], o_sem.at[0]).start()
                else:
                    a[:width, :] = jnp.zeros((width, cols), F32)
                    proj[...] = jnp.zeros_like(proj)
                    v_own(k + 1).wait()
                    project(k + 1, 0)
            for piece in range(CHUNKS):
                take_level(k, level, piece)
                if level + 1 < levels:
                    send_level(k, level + 1, piece)

    head_rows = pl.ds(0, width)
    pltpu.make_async_copy(top, o_ref.at[head_rows], o_top_sem).start()

    for k in range(panels):
        for mask in masks:
            v_copy(k, mask).wait_send()
    for which in range(3):
        for mask in masks:
            small_copy(which, small_in[which], mask).wait_send()
    for level in range(levels):
        @pl.when(is_lower(level))
        def _():
            s_copy(level).wait_send()

        @pl.when(takes_part(level))
        def _():
            for k in range(panels):
                for piece in range(CHUNKS):
                    x_copy(k, level, piece).wait_send()
    rest = pl.ds(width, TILE - width)
    pltpu.make_async_copy(a.at[rest], o_ref.at[rest], o_sem.at[0]).wait()
    for t in range(1, tiles):
        at = pl.ds(t * TILE, TILE)
        pltpu.make_async_copy(a.at[at], o_ref.at[at], o_sem.at[t]).wait()
    pltpu.make_async_copy(top, o_ref.at[head_rows], o_top_sem).wait()


def local(n_row, n_col, matrix, leaf_vectors, leaf_factors, tree_vectors, tree_factors):
    rows, cols = matrix.shape
    panels, shard, width = leaf_vectors.shape
    levels = n_row.bit_length() - 1
    chunk = cols // CHUNKS
    anywhere = pl.BlockSpec(memory_space=pl.ANY)
    dma = pltpu.SemaphoreType.DMA
    return pl.pallas_call(
        functools.partial(kernel, n_row, n_col),
        out_shape=jax.ShapeDtypeStruct((rows, cols), F32),
        in_specs=[anywhere] * 5,
        out_specs=anywhere,
        scratch_shapes=[
            pltpu.VMEM((rows, cols), F32),
            pltpu.VMEM((panels, rows, width), F32),
            pltpu.VMEM((rows, 2 * width), BF16),
            pltpu.VMEM((3, panels, width, width), F32),
            pltpu.VMEM((levels, panels, width, width), F32),
            pltpu.VMEM((width, cols), F32),
            pltpu.VMEM((width, cols), F32),
            pltpu.VMEM((2 * width, cols), BF16),
            pltpu.VMEM((width, cols), BF16),
            pltpu.VMEM((panels, levels, CHUNKS, width, chunk), F32),
            pltpu.VMEM((panels, levels, CHUNKS, width, chunk), F32),
            dma((n_col,)),
            dma((panels,)),
            dma((panels, n_col)),
            dma((panels, n_col)),
            dma((3,)),
            dma((3, n_col)),
            dma((3, n_col)),
            dma((levels,)),
            dma((levels,)),
            dma((panels, levels, CHUNKS)),
            dma((panels, levels, CHUNKS)),
            dma((rows // TILE,)),
            dma(()),
        ],
        compiler_params=pltpu.CompilerParams(
            collective_id=0, has_side_effects=True, vmem_limit_bytes=56 << 20
        ),
    )(matrix, leaf_vectors, leaf_factors, tree_vectors, tree_factors)


def solution(mesh):
    placed = (
        P("row", "col"),
        P(None, ("row", "col"), None),
        P(None, ("row", "col"), None),
        P(None, ("row", "col"), None),
        P(None, ("row", "col"), None),
    )
    return jax.shard_map(
        functools.partial(local, mesh.shape["row"], mesh.shape["col"]),
        mesh=mesh, in_specs=placed, out_specs=P("row", "col"), check_vma=False,
    )
```

time: 259 us -> 101 us (0.39); the launches traced: 254 us -> 101 us
  Pallas kernels: 0 us -> 92.9 us
  matrix products: 71.5 us -> 0 us
  waiting for transfers between devices: 49.6 us -> 0 us
  local copies, waits for them, and re-layouts: 47.3 us -> 7.76 us
  starting transfers between devices: 35.3 us -> 0 us
  blocking collectives: 29.1 us -> 0 us
  between operations: 13.9 us -> 0.01 us
  other arithmetic: 7.73 us -> 0 us
    pallas_call x0 -> x1, Pallas kernels: none -> 92.9 us  [local(): pl.pallas_call(functools.partial(kernel, n_row, n_col), out_shape=jax.Sha...]
    dot_general x36 -> x0, matrix products: 71.5 us -> none  [the longest x24 40.3 us: transposed_dot(): lax.dot_general(left, right, (((0,), (0,)), ((), ())), precision=lax.Prec...]
    ppermute x27 -> x0, waiting for transfers between devices: 49.5 us -> none  [swapped(): return lax.ppermute(block, axis, route)]
    ppermute x27 -> x0, starting transfers between devices: 35.2 us -> none  [swapped(): return lax.ppermute(block, axis, route)]
    all_gather x5 -> x0, blocking collectives: 29.1 us -> none  [the longest x3 16.4 us: local(): lax.all_gather(leaf_factors[tick_index], 'col', axis=0, tiled=True)]
    slice x8 -> x0, local copies, waits for them, and re-layouts: 24.9 us -> none  [the longest x3 21.4 us: local(): trailing = jnp.concatenate([top_rows, trailing[block_width:]], axis=0)]
    concatenate x1 -> x0, local copies, waits for them, and re-layouts: 8.94 us -> none  [local(): trailing = jnp.concatenate([top_rows, trailing[block_width:]], axis=0)]
    concatenate x1 -> x0, other arithmetic: 7.63 us -> none  [local(): trailing = jnp.concatenate([top_rows, trailing[block_width:]], axis=0)]
  transfers between devices with their start and end apart: 30 -> 0, of which waited for: 15 -> 0; matrix products, arithmetic and copies ran while one was open for 32% -> 0% of each run, Pallas kernels for 0% -> 0%
where the time goes in v1:
time: 101 us
  Pallas kernels  92.9 us (92%)
  local copies, waits for them, and re-layouts  7.76 us (8%)
    pallas_call x1, Pallas kernels, local(): pl.pallas_call(functools.partial(kernel, n_row, n_col), out_shape=jax.Sha...  92.9 us
    unnamed x1, local copies, waits for them, and re-layouts  7.76 us

profile of v1, /device:TPU:0, one launch (start us, length us, event | category | flops | bytes accessed | tf_op | source)
XLA Modules:
  0.0 100.7 jit_solution(13649933922061692774)
XLA Ops:
  0.0 92.9 %shard_map.55 = f32[4096,512]{1,0:T(8,128)} custom-call(f32[4096,512]{1,0:T(8,128)} %a_in.1, f32[3,1024,128]{2,1,0:T(8,128)} %v_in.1, f32[3,32,128]{2,1,0:T(8,128)} %l_in.1, f32[3,32,128]{2,1,0:T(8,128)} %y_in.1, f32[3,32,128]{2,1,0:T(8,128)} %s_in.1), custom_call_target="tpu_custom_call" | custom-call | tf_op jit(solution)/shard_map/pallas_call | solution.py:350
  92.9 7.8 %copy.7 = f32[4096,512]{1,0:T(8,128)} copy(f32[4096,512]{1,0:T(8,128)} %shard_map.55) | data formatting | bytes 16777216

commit v2 on v1

--- a/solution.py
+++ b/solution.py
@@ -104,13 +104,16 @@
             source, small.at[which, :, part_rows(0)], small_own.at[which]
         )
 
-    def small_copy(which, source, mask):
+    def small_copy(which, mask):
+        bit = low_bit(mask)
+        held = mask ^ bit
+        there = small.at[which, :, part_rows(held)]
         return pltpu.make_async_remote_copy(
-            src_ref=source,
-            dst_ref=small.at[which, :, part_rows(0)],
+            src_ref=small_in[which] if held == 0 else there,
+            dst_ref=there,
             send_sem=small_send.at[which, mask],
             recv_sem=small_recv.at[which, mask],
-            device_id={"row": r, "col": partner(mask)},
+            device_id={"row": r, "col": partner(bit)},
             device_id_type=MESH,
         )
 
@@ -144,6 +147,8 @@
         return r % (1 << level) == 0
 
     masks = range(1, n_col)
+    direct = [mask for mask in masks if mask == low_bit(mask)]
+    relayed = [mask for mask in masks if mask != low_bit(mask)]
     small_in = (l_in, y_in, s_in)
 
     for mask in range(n_col):
@@ -176,8 +181,8 @@
     start_near(0)
     start_far(0)
     for which in range(3):
-        for mask in masks:
-            small_copy(which, small_in[which], mask).start()
+        for mask in direct:
+            small_copy(which, mask).start()
     for k in range(1, panels):
         start_near(k)
 
@@ -243,6 +248,14 @@
             total = sent[k, level, piece] + got[k, level, piece]
             top[:, columns(piece)] -= dot3(upper_triangle(lower_s[level, k]), total, 0)
 
+    def relay_small(mask):
+        for which in range(3):
+            small_copy(which, mask).wait_recv()
+            bit = 1
+            while bit < low_bit(mask):
+                small_copy(which, mask | bit).start()
+                bit *= 2
+
     def receive(k, mask):
         v_copy(k, mask).wait_recv()
         bit = 1
@@ -251,8 +264,7 @@
             bit *= 2
 
     last_direct = n_col // 2
-    order = [mask for mask in masks if mask == low_bit(mask)]
-    order += [mask for mask in masks if mask != low_bit(mask)]
+    order = direct + relayed
 
     proj[...] = jnp.zeros_like(proj)
     a_copy(0).wait()
@@ -266,13 +278,12 @@
                 start_far(k + 1)
             if k == 0:
                 a_copy(mask).wait()
+                relay_small(mask)
             project(k, mask)
         if k == 0:
             top[...] = a[:width, :]
             for which in range(3):
                 small_local(which, small_in[which]).wait()
-                for mask in masks:
-                    small_copy(which, small_in[which], mask).wait_recv()
             for level in range(levels):
                 @pl.when(is_lower(level))
                 def _():
@@ -321,7 +332,7 @@
             v_copy(k, mask).wait_send()
     for which in range(3):
         for mask in masks:
-            small_copy(which, small_in[which], mask).wait_send()
+            small_copy(which, mask).wait_send()
     for level in range(levels):
         @pl.when(is_lower(level))
         def _():

time: 101 us -> 99.1 us (0.981)
  Pallas kernels: 92.9 us -> 91.2 us
    pallas_call x1, Pallas kernels: 92.9 us -> 91.2 us  [local(): pl.pallas_call(functools.partial(kernel, n_row, n_col), out_shape=jax.Sha...]
where the time goes in v2:
time: 99.1 us; the launch traced here: 98.9 us
  Pallas kernels  91.2 us (92%)
  local copies, waits for them, and re-layouts  7.76 us (8%)
    pallas_call x1, Pallas kernels, local(): pl.pallas_call(functools.partial(kernel, n_row, n_col), out_shape=jax.Sha...  91.2 us
    unnamed x1, local copies, waits for them, and re-layouts  7.76 us

profile of v2, /device:TPU:0, one launch (start us, length us, event | category | flops | bytes accessed | tf_op | source)
XLA Modules:
  0.0 98.9 jit_solution(5313611807035439576)
XLA Ops:
  0.0 91.2 %shard_map.55 = f32[4096,512]{1,0:T(8,128)} custom-call(f32[4096,512]{1,0:T(8,128)} %a_in.1, f32[3,1024,128]{2,1,0:T(8,128)} %v_in.1, f32[3,32,128]{2,1,0:T(8,128)} %l_in.1, f32[3,32,128]{2,1,0:T(8,128)} %y_in.1, f32[3,32,128]{2,1,0:T(8,128)} %s_in.1), custom_call_target="tpu_custom_call" | custom-call | tf_op jit(solution)/shard_map/pallas_call | solution.py:361
  91.2 7.8 %copy.7 = f32[4096,512]{1,0:T(8,128)} copy(f32[4096,512]{1,0:T(8,128)} %shard_map.55) | data formatting | bytes 16777216
